TPU v7x, 256 devices: a whole 4x4x8 slice. The times are simulated.
256 devices in a mesh: gx: 16 (over y, x), gy: 8 (over z), gz: 2 (over core).
Axes of the slice: x: 4, y: 4, z: 8, core: 2. Of those that a mesh axis runs over, the one named last changes fastest.
Arguments:
- tokens_in: bfloat16 [2048, 12288], P('gx', ('gz', 'gy')), may hold values from -20.4 to 20.4
- qkv_weight: bfloat16 [96, 128, 64, 384], P('gz', 'gx', 'gy'), may hold values from -0.0546875 to 0.0546875
- qkv_mask: int32 [96, 64, 3], P('gz', 'gy'), may hold values from 0 to 1, as said below
- out_weight: bfloat16 [64, 128, 12288], P('gy', 'gx', 'gz'), may hold values from -0.0625 to 0.0625
- out_mask: int32 [64, 96], P('gy', 'gz'), may hold values from 0 to 1, as said below
Outputs:
- mixed: bfloat16 [2048, 12288], P(('gx', 'gy'), 'gz')
Inputs may be any that keep to these rules, and one draw needn't show every extreme that they name: `qkv_mask`: exactly half of the blocks are kept within each face of 48 row blocks by 8 heads by 3 (row blocks r * 48 to r * 48 + 47, heads g * 8 to g * 8 + 7). `out_mask`: exactly half of the blocks are kept within each face of 8 heads by 48 column blocks, aligned as for qkv_mask.
All inputs are finite; a program needn't handle non-finite values.
Results may differ from a plain program's by a relative error of at most 0.005.
The roundings to bfloat16 on the way count: a program that leaves them out, or rounds other values in their place, can miss the bound.
Values may be sent and summed in bfloat16 or wider, within the bound.
No kernel may reach another device: no remote copies, remote signals or barrier semaphores. Data moves between devices by JAX's collectives and lax.ppermute only.
A program may use at most 192 MiB of HBM per device.

v0:
```python
import jax
import jax.numpy as jnp
from jax import lax
from jax.sharding import PartitionSpec as P

HEAD = 128
BLOCK = 128


def body(tokens_in, qkv_weight, qkv_mask, out_weight, out_mask):
    features = lax.all_gather(tokens_in, "gy", axis=1, tiled=True)
    tok_rows = features.shape[0]
    row_blocks, sub_rows, group_heads, triple = qkv_weight.shape
    full_tiles = lax.all_gather(qkv_weight, "gx", axis=1, tiled=True)
    keep_qkv = qkv_mask.astype(jnp.bfloat16)[:, None, :, :, None]
    masked = full_tiles.reshape(row_blocks, BLOCK, group_heads, 3, HEAD) * keep_qkv
    masked = masked.reshape(row_blocks * BLOCK, group_heads * triple)
    partial_value = jnp.dot(features, masked, preferred_element_type=jnp.float32)
    partial_value = partial_value.reshape(tok_rows, group_heads, triple)
    own_heads = lax.psum_scatter(partial_value, "gz", scatter_dimension=1, tiled=True).astype(
        jnp.bfloat16
    )
    queries = own_heads[:, :, :HEAD]
    keys_mine = own_heads[:, :, HEAD : 2 * HEAD]
    values_mine = own_heads[:, :, 2 * HEAD :]
    keys_all, values_all = (
        lax.all_gather(keys_mine, "gx", axis=0, tiled=True),
        lax.all_gather(values_mine, "gx", axis=0, tiled=True),
    )
    total_tokens = keys_all.shape[0]
    offset = lax.axis_index("gx") * tok_rows
    scores = jnp.einsum(
        "qhd,khd->hqk", queries, keys_all, preferred_element_type=jnp.float32
    ) * HEAD ** (-0.5)
    query_pos = offset + jnp.arange(tok_rows)
    key_pos = jnp.arange(total_tokens)
    allowed = key_pos[None, :] <= query_pos[:, None]
    scores = jnp.where(allowed[None], scores, -1e30)
    row_top = jnp.max(scores, axis=2, keepdims=True)
    weights = jnp.exp(scores - row_top)
    normed = (weights / jnp.sum(weights, axis=2, keepdims=True)).astype(jnp.bfloat16)
    attended = jnp.einsum(
        "hqk,khd->qhd", normed, values_all, preferred_element_type=jnp.float32
    ).astype(jnp.bfloat16)
    gathered = lax.all_gather(attended, "gz", axis=1, tiled=True)
    out_heads, out_sub, out_cols = out_weight.shape
    col_blocks = out_cols // BLOCK
    out_full = lax.all_gather(out_weight, "gx", axis=1, tiled=True)
    keep_out = out_mask.astype(jnp.bfloat16)[:, None, :, None]
    out_masked = out_full.reshape(out_heads, HEAD, col_blocks, BLOCK) * keep_out
    flat_in = gathered.reshape(tok_rows, out_heads * HEAD)
    summed = jnp.dot(
        flat_in, out_masked.reshape(out_heads * HEAD, out_cols), preferred_element_type=jnp.float32
    )
    return lax.psum_scatter(summed, "gy", scatter_dimension=0, tiled=True).astype(jnp.bfloat16)


def solution(mesh):
    return jax.shard_map(
        body,
        mesh=mesh,
        in_specs=(
            P("gx", ("gz", "gy")),
            P("gz", "gx", "gy", None),
            P("gz", "gy", None),
            P("gy", "gx", "gz"),
            P("gy", "gz"),
        ),
        out_specs=P(("gx", "gy"), "gz"),
        check_vma=False,
    )
```

profile of v0, /device:TPU:4, one launch (start us, length us, event | category | flops | bytes accessed | tf_op | source)
XLA Modules:
  0.0 631.0 jit_solution(10556620752532145886)
XLA Ops:
  6.5 0.0 all-gather.6.cloned.1.call-start
  6.5 0.7 all-gather.6.cloned.1.call-update
  7.3 0.0 all-gather.8.cloned.1.call-start
  7.3 0.7 all-gather.8.cloned.1.call-update
  8.0 0.0 reduce-scatter.3.cloned.1.call-start
  8.1 0.7 convert_element_type.21
  8.8 227.4 %all-gather.6.cloned.1.call-done = bf16[48,128,8,384]{3,2,1,0:T(8,128)(2,1)} async-done(((bf16[48,8,8,384]{3,2,1,0:T(8,128)(2,1)}), bf16[48,128,8,384]{3,2,1,0:T(8,128)(2,1)}) %all-gather.6.cloned.1.call-update) | async-done | bytes 37748752 | tf_op jit(solution)/shard_map/all_gather | solution.py:14
  236.2 25.3 %copy.21 = bf16[768,8,8,384]{3,1,2,0:T(8,128)(2,1)} copy(bf16[768,8,8,384]{3,2,1,0:T(8,128)(2,1)} %bitcast.25) | data formatting | bytes 75497472
  261.4 48.7 %copy.20 = bf16[6144,3072]{0,1:T(8,128)(2,1)} copy(bf16[6144,3072]{1,0:T(8,128)(2,1)} %bitcast.23) | data formatting | bytes 75497472 | tf_op jit(solution)/shard_map/reshape | solution.py:16
  310.2 0.0 all-gather.8.cloned.1.call-done
  310.2 0.0 copy-start.1
  310.2 12.6 %mul.34 = bf16[48,128,8,3,128]{1,0,4,3,2:T(8,128)(2,1)} broadcast(bf16[48,8,3]{0,2,1:T(4,128)(2,1)S(1)} %copy.14), dimensions={0,2,3} | broadcast | bytes 37751040 | tf_op jit(solution)/shard_map/mul | solution.py:16
  322.8 0.0 copy-done.1
  322.8 26.7 %fusion.1 = f32[3072,128]{1,0:T(8,128)S(1)} fusion(bf16[128,6144]{1,0:T(8,128)(2,1)S(1)} %copy-done.1, bf16[6144,3072]{0,1:T(8,128)(2,1)} %copy.20, bf16[384,8,48,128]{3,2,1,0:T(8,128)(2,1)} %bitcast.24), kind=kOutput, calls=%fused_computation.2 | convolution fusion | flops 4850712576 | bytes 78643200 | tf_op jit(solution)/shard_map/dot_general | solution.py:18
  349.5 0.0 copy-start
  349.5 1.6 copy.15
  351.1 0.0 reduce-scatter.3.cloned.1.call-update
  351.2 0.0 all-gather.12.cloned.1.call-start
  351.2 14.4 %reduce-scatter.3.cloned.1.call-done = f32[128,4,384]{2,0,1:T(8,128)} async-done(((f32[128,8,384]{2,0,1:T(8,128)}), f32[128,4,384]{2,0,1:T(8,128)}) %reduce-scatter.3.cloned.1.call-update) | async-done | bytes 786448 | tf_op jit(solution)/shard_map/reduce_scatter | solution.py:20
  365.6 1.2 convert_element_type.22
  366.8 0.7 fusion.26
  367.5 0.0 all-gather.12.cloned.1.call-update
  367.5 0.0 all-gather.10.cloned.1.call-start
  367.6 0.5 all-gather.10.cloned.1.call-update
  368.1 0.0 all-gather.14.cloned.1.call-start
  368.2 0.5 all-gather.14.cloned.1.call-update
  368.7 0.0 reduce-scatter.5.cloned.1.call-start
  368.8 0.0 copy-done
  368.8 0.1 copy.18
  368.9 0.2 iota_compare_fusion
  369.1 0.1 broadcast_bitcast_fusion
  369.2 49.0 %all-gather.12.cloned.1.call-done = bf16[2048,4,128]{2,0,1:T(8,128)(2,1)} async-done(((bf16[128,4,128]{2,0,1:T(8,128)(2,1)}), bf16[2048,4,128]{2,0,1:T(8,128)(2,1)}) %all-gather.12.cloned.1.call-update) | async-done | bytes 2097168 | tf_op jit(solution)/shard_map/all_gather | solution.py:27
  418.2 5.1 fusion.27
  423.3 46.6 %all-gather.10.cloned.1.call-done = bf16[2048,4,128]{2,0,1:T(8,128)(2,1)} async-done(((bf16[128,4,128]{2,0,1:T(8,128)(2,1)}), bf16[2048,4,128]{2,0,1:T(8,128)(2,1)}) %all-gather.10.cloned.1.call-update) | async-done | bytes 2097168 | tf_op jit(solution)/shard_map/all_gather | solution.py:28
  469.9 3.8 fusion.15
  473.6 0.1 copy.17
  473.8 2.0 all_gather.22
  475.8 91.5 %all-gather.14.cloned.1.call-done = bf16[8,128,6144]{2,1,0:T(8,128)(2,1)} async-done(((bf16[8,8,6144]{2,1,0:T(8,128)(2,1)}), bf16[8,128,6144]{2,1,0:T(8,128)(2,1)}) %all-gather.14.cloned.1.call-update) | async-done | bytes 12582928 | tf_op jit(solution)/shard_map/all_gather | solution.py:48
  567.3 8.0 %fusion.5 = f32[128,6144]{1,0:T(8,128)} fusion(bf16[128,8,128]{2,0,1:T(8,128)(2,1)S(1)} %all_gather.22, bf16[8,128,6144]{2,1,0:T(8,128)(2,1)} %all-gather.14.cloned.1.call-done, bf16[8,6144]{1,0:T(8,128)(2,1)S(1)} %broadcast_bitcast_fusion), kind=kOutput, calls=%fused_computation.6 | convolution fusion | flops 1616904192 | bytes 16089088 | tf_op jit(solution)/shard_map/dot_general | solution.py:52
  575.3 0.0 reduce-scatter.5.cloned.1.call-update
  575.4 47.1 %reduce-scatter.5.cloned.1.call-done = f32[16,6144]{1,0:T(8,128)} async-done(((f32[128,6144]{1,0:T(8,128)}), f32[16,6144]{1,0:T(8,128)}) %reduce-scatter.5.cloned.1.call-update) | async-done | bytes 393232 | tf_op jit(solution)/shard_map/reduce_scatter | solution.py:55
  622.4 1.7 convert_element_type.27
  (3 shorter events, 0.0 us)
Async XLA Ops:
  6.5 229.6 %all-gather.6.cloned.1.call-start = ((), (), s32[]{:S(2)}) async-start(), calls=%async_computation.2 | async-start | bytes 40108032 | tf_op jit(solution)/shard_map/all_gather | solution.py:14
  7.3 302.9 %all-gather.8.cloned.1.call-start = ((), (), s32[]{:S(2)}) async-start(), calls=%async_computation.3 | async-start | bytes 1769472 | tf_op jit(solution)/shard_map/all_gather | solution.py:11
  8.0 357.6 %reduce-scatter.3.cloned.1.call-start = ((), (), s32[]{:S(2)}) async-start(), calls=%async_computation.4 | async-start | bytes 2359296 | tf_op jit(solution)/shard_map/reduce_scatter | solution.py:20
  310.2 12.6 %copy-start.1 = (bf16[128,6144]{1,0:T(8,128)(2,1)S(1)}, bf16[128,6144]{1,0:T(8,128)(2,1)}, u32[]{:S(2)}) copy-start(bf16[128,6144]{1,0:T(8,128)(2,1)} %all-gather.8.cloned.1.call-done) | copy-start | bytes 4718596
  349.5 19.3 %copy-start = (s32[8,48]{1,0:T(8,128)S(1)}, s32[8,48]{1,0:T(8,128)}, u32[]{:S(2)}) copy-start(s32[8,48]{1,0:T(8,128)} %param.9) | copy-start | bytes 4612
  351.2 67.1 %all-gather.12.cloned.1.call-start = ((), (), s32[]{:S(2)}) async-start(), calls=%async_computation.6 | async-start | bytes 2228224 | tf_op jit(solution)/shard_map/all_gather | solution.py:27
  367.5 102.3 %all-gather.10.cloned.1.call-start = ((), (), s32[]{:S(2)}) async-start(), calls=%async_computation.5 | async-start | bytes 2228224 | tf_op jit(solution)/shard_map/all_gather | solution.py:28
  368.1 199.2 %all-gather.14.cloned.1.call-start = ((), (), s32[]{:S(2)}) async-start(), calls=%async_computation.7 | async-start | bytes 13369344 | tf_op jit(solution)/shard_map/all_gather | solution.py:48
  368.7 253.7 %reduce-scatter.5.cloned.1.call-start = ((), (), s32[]{:S(2)}) async-start(), calls=%async_computation.8 | async-start | bytes 3538944 | tf_op jit(solution)/shard_map/reduce_scatter | solution.py:55
Sparse Core Ops, SparseCore 0:
  9.8 226.3 all-gather.5
  237.9 39.2 all-gather.7
  351.3 14.2 reduce-scatter.2
  367.9 50.2 all-gather.11
  420.5 49.3 all-gather.9
  472.1 95.1 all-gather.13
  575.5 46.9 reduce-scatter.4
where the time goes:
time: 632 us; the launch traced here: 631 us
  waiting for transfers between devices  478 us (76%)
  local copies, waits for them, and re-layouts  89.3 us (14%)
  matrix products  43.6 us (7%)
  between operations  13.6 us (2%)
    all_gather x1, waiting for transfers between devices, body(): full_tiles = lax.all_gather(qkv_weight, 'gx', axis=1, tiled=True)  227 us
    all_gather x1, waiting for transfers between devices, body(): out_full = lax.all_gather(out_weight, 'gx', axis=1, tiled=True)  91.5 us
    all_gather x1, waiting for transfers between devices, body(): lax.all_gather(keys_mine, 'gx', axis=0, tiled=True)  49 us
    reshape x1, local copies, waits for them, and re-layouts, body(): full_tiles.reshape(row_blocks, BLOCK, group_heads, 3, HEAD) * keep_qkv  48.7 us
    reduce_scatter x1, waiting for transfers between devices, body(): lax.psum_scatter(summed, 'gy', scatter_dimension=0, tiled=True)  47.1 us
    all_gather x1, waiting for transfers between devices, body(): lax.all_gather(values_mine, 'gx', axis=0, tiled=True)  46.6 us
    dot_general x1, matrix products, body(): jnp.dot(features, masked, preferred_element_type=jnp.float32)  26.7 us
    unnamed x5, local copies, waits for them, and re-layouts  25.3 us
  transfers between devices with their start and end apart: 7, of which 6 were waited for; matrix products, arithmetic and copies ran while one was open for 13% of the time, Pallas kernels for 0%

commit v1 on v0

--- a/solution.py
+++ b/solution.py
@@ -1,3 +1,4 @@
+import functools
 import jax
 import jax.numpy as jnp
 from jax import lax
@@ -5,6 +6,16 @@
 
 HEAD = 128
 BLOCK = 128
+
+
+def _recover_things(my_data, which_axis):
+    piece_now = lax.axis_size(which_axis)
+    y_new = jnp.stack([my_data] * piece_now)
+    x_now = lax.all_to_all(y_new, axis_name=which_axis, split_axis=0, concat_axis=0)
+    return jnp.concatenate(x_now, axis=1)
+
+
+leaf_produce = functools.partial(_recover_things, which_axis="gx")
 
 
 def body(tokens_in, qkv_weight, qkv_mask, out_weight, out_mask):
@@ -45,7 +56,7 @@
     gathered = lax.all_gather(attended, "gz", axis=1, tiled=True)
     out_heads, out_sub, out_cols = out_weight.shape
     col_blocks = out_cols // BLOCK
-    out_full = lax.all_gather(out_weight, "gx", axis=1, tiled=True)
+    out_full = leaf_produce(out_weight)
     keep_out = out_mask.astype(jnp.bfloat16)[:, None, :, None]
     out_masked = out_full.reshape(out_heads, HEAD, col_blocks, BLOCK) * keep_out
     flat_in = gathered.reshape(tok_rows, out_heads * HEAD)

time: 632 us -> 691 us (1.093)
  waiting for transfers between devices: 478 us -> 512 us
  other arithmetic: 3.81 us -> 13.6 us
  local copies, waits for them, and re-layouts: 89.3 us -> 97 us
  starting transfers between devices: 0.24 us -> 7.78 us
    all_gather x1, waiting for transfers between devices: 227 us -> 358 us  [body(): full_tiles = lax.all_gather(qkv_weight, 'gx', axis=1, tiled=True)]
    all_gather x1 -> x0, waiting for transfers between devices: 91.5 us -> none  [body(): out_full = lax.all_gather(out_weight, 'gx', axis=1, tiled=True)]
    mul x0 -> x1, other arithmetic: none -> 10.5 us  [body(): out_masked = out_full.reshape(out_heads, HEAD, col_blocks, BLOCK) * keep_out]
    all_gather x1, waiting for transfers between devices: 49 us -> 39.1 us  [body(): lax.all_gather(keys_mine, 'gx', axis=0, tiled=True)]
    all_to_all x0 -> x1, starting transfers between devices: none -> 7.58 us  [_recover_things(): lax.all_to_all(y_new, axis_name=which_axis, split_axis=0, concat_axis=0)]
    another operation x0 -> x1, local copies, waits for them, and re-layouts: none -> 7.32 us  [_recover_things(): y_new = jnp.stack([my_data] * piece_now)]
    unnamed x5 -> x7, local copies, waits for them, and re-layouts: 25.3 us -> 25.4 us
  transfers between devices with their start and end apart: 7 -> 7, of which waited for: 6 -> 5; matrix products, arithmetic and copies ran while one was open for 13% -> 20% of each run, Pallas kernels for 0% -> 0%
where the time goes in v1:
time: 691 us; the launch traced here: 689 us
  waiting for transfers between devices  512 us (74%)
  local copies, waits for them, and re-layouts  97 us (14%)
  matrix products  43.6 us (6%)
  other arithmetic  13.6 us (2%)
  between operations  13.6 us (2%)
  starting transfers between devices  7.78 us (1%)
    all_gather x1, waiting for transfers between devices, body(): full_tiles = lax.all_gather(qkv_weight, 'gx', axis=1, tiled=True)  358 us
    reshape x1, local copies, waits for them, and re-layouts, body(): full_tiles.reshape(row_blocks, BLOCK, group_heads, 3, HEAD) * keep_qkv  48.7 us
    reduce_scatter x1, waiting for transfers between devices, body(): lax.psum_scatter(summed, 'gy', scatter_dimension=0, tiled=True)  47.6 us
    all_gather x1, waiting for transfers between devices, body(): lax.all_gather(values_mine, 'gx', axis=0, tiled=True)  46.6 us
    all_gather x1, waiting for transfers between devices, body(): lax.all_gather(keys_mine, 'gx', axis=0, tiled=True)  39.1 us
    dot_general x1, matrix products, body(): jnp.dot(features, masked, preferred_element_type=jnp.float32)  26.7 us
    unnamed x7, local copies, waits for them, and re-layouts  25.4 us
    reduce_scatter x1, waiting for transfers between devices, body(): lax.psum_scatter(partial_value, 'gz', scatter_dimension=1, tiled=True)  18.3 us
  transfers between devices with their start and end apart: 7, of which 5 were waited for; matrix products, arithmetic and copies ran while one was open for 20% of the time, Pallas kernels for 0%

profile of v1, /device:TPU:4, one launch (start us, length us, event | category | flops | bytes accessed | tf_op | source)
XLA Modules:
  0.0 689.2 jit_solution(16229127853399805226)
XLA Ops:
  6.5 0.0 all-gather.5.cloned.1.call-start
  6.5 0.7 all-gather.5.cloned.1.call-update
  7.3 0.0 all-gather.7.cloned.1.call-start
  7.3 0.7 all-gather.7.cloned.1.call-update
  8.0 7.3 %stack.2 = bf16[16,8,8,6144]{3,2,1,0:T(8,128)(2,1)} broadcast(bf16[8,8,6144]{2,1,0:T(8,128)(2,1)} %param.8), dimensions={1,2,3} | broadcast | bytes 13369344 | tf_op jit(solution)/shard_map/stack | solution.py:13
  15.3 0.0 copy-start
  15.3 7.6 %all-to-all-start = ((bf16[16,8,8,6144]{3,2,1,0:T(8,128)(2,1)}), bf16[16,8,8,6144]{3,2,1,0:T(8,128)(2,1)}, u32[]{:S(2)}, u32[]{:S(2)}) async-start(bf16[16,8,8,6144]{3,2,1,0:T(8,128)(2,1)} %stack.2), calls=%async_computation.1 | async-start | bytes 25165824 | tf_op jit(solution)/shard_map/all_to_all | solution.py:14
  22.9 0.0 reduce-scatter.3.cloned.1.call-start
  23.0 0.0 copy-done
  23.0 358.1 %all-gather.5.cloned.1.call-done = bf16[48,128,8,384]{3,2,1,0:T(8,128)(2,1)} async-done(((bf16[48,8,8,384]{3,2,1,0:T(8,128)(2,1)}), bf16[48,128,8,384]{3,2,1,0:T(8,128)(2,1)}) %all-gather.5.cloned.1.call-update) | async-done | bytes 37748752 | tf_op jit(solution)/shard_map/all_gather | solution.py:25
  381.1 25.4 %copy.32 = bf16[768,8,8,384]{3,1,2,0:T(8,128)(2,1)} copy(bf16[768,8,8,384]{3,2,1,0:T(8,128)(2,1)} %bitcast.29) | data formatting | bytes 75497472
  406.5 48.7 %copy.31 = bf16[6144,3072]{0,1:T(8,128)(2,1)} copy(bf16[6144,3072]{1,0:T(8,128)(2,1)} %bitcast.26) | data formatting | bytes 75497472 | tf_op jit(solution)/shard_map/reshape | solution.py:27
  455.2 0.0 all-gather.7.cloned.1.call-done
  455.2 0.0 copy-start.2
  455.2 12.6 %mul.39 = bf16[48,128,8,3,128]{1,0,4,3,2:T(8,128)(2,1)} broadcast(bf16[48,8,3]{0,2,1:T(4,128)(2,1)S(1)} %copy.23), dimensions={0,2,3} | broadcast | bytes 37751040 | tf_op jit(solution)/shard_map/mul | solution.py:27
  467.8 0.0 copy-done.2
  467.8 26.7 %fusion.1 = f32[3072,128]{1,0:T(8,128)S(1)} fusion(bf16[128,6144]{1,0:T(8,128)(2,1)S(1)} %copy-done.2, bf16[6144,3072]{0,1:T(8,128)(2,1)} %copy.31, bf16[384,8,48,128]{3,2,1,0:T(8,128)(2,1)} %bitcast.28), kind=kOutput, calls=%fused_computation.2 | convolution fusion | flops 4850712576 | bytes 78643200 | tf_op jit(solution)/shard_map/dot_general | solution.py:29
  494.5 0.0 copy-start.1
  494.5 1.6 copy.24
  496.2 0.0 reduce-scatter.3.cloned.1.call-update
  496.2 0.0 all-gather.11.cloned.1.call-start
  496.2 18.3 %reduce-scatter.3.cloned.1.call-done = f32[128,4,384]{2,0,1:T(8,128)} async-done(((f32[128,8,384]{2,0,1:T(8,128)}), f32[128,4,384]{2,0,1:T(8,128)}) %reduce-scatter.3.cloned.1.call-update) | async-done | bytes 786448 | tf_op jit(solution)/shard_map/reduce_scatter | solution.py:31
  514.5 1.2 convert_element_type.22
  515.7 0.7 fusion.20
  516.4 0.0 all-gather.11.cloned.1.call-update
  516.5 0.0 all-gather.9.cloned.1.call-start
  516.5 0.5 all-gather.9.cloned.1.call-update
  517.1 0.0 reduce-scatter.5.cloned.1.call-start
  517.1 0.2 iota_compare_fusion
  517.3 0.0 copy-done.1
  517.4 0.1 copy.28
  517.5 0.1 broadcast_bitcast_fusion
  517.6 0.0 all-to-all-done
  517.6 10.5 %copy_multiply_fusion = bf16[16,8,8,6144]{3,2,0,1:T(8,128)(2,1)} fusion(bf16[16,8,8,6144]{3,2,1,0:T(8,128)(2,1)} %all-to-all-done, bf16[8,6144]{1,0:T(8,128)(2,1)S(1)} %broadcast_bitcast_fusion), kind=kLoop, calls=%fused_computation.4 | loop fusion | flops 6291456 | bytes 25264128 | tf_op jit(solution)/shard_map/mul | solution.py:61
  528.1 39.1 %all-gather.11.cloned.1.call-done = bf16[2048,4,128]{2,0,1:T(8,128)(2,1)} async-done(((bf16[128,4,128]{2,0,1:T(8,128)(2,1)}), bf16[2048,4,128]{2,0,1:T(8,128)(2,1)}) %all-gather.11.cloned.1.call-update) | async-done | bytes 2097168 | tf_op jit(solution)/shard_map/all_gather | solution.py:38
  567.2 5.1 fusion.21
  572.2 46.6 %all-gather.9.cloned.1.call-done = bf16[2048,4,128]{2,0,1:T(8,128)(2,1)} async-done(((bf16[128,4,128]{2,0,1:T(8,128)(2,1)}), bf16[2048,4,128]{2,0,1:T(8,128)(2,1)}) %all-gather.9.cloned.1.call-update) | async-done | bytes 2097168 | tf_op jit(solution)/shard_map/all_gather | solution.py:39
  618.8 3.8 fusion.9
  622.6 0.1 copy.26
  622.7 2.0 all_gather.19
  624.7 0.2 copy.27
  624.9 8.1 %fusion.24 = f32[128,6144]{1,0:T(8,128)} fusion(bf16[128,1024]{0,1:T(8,128)(2,1)S(1)} %bitcast.31, bf16[1024,6144]{1,0:T(8,128)(2,1)} %bitcast.27), kind=kOutput, calls=%fused_computation.26 | convolution fusion | flops 1610612736 | bytes 15990784 | tf_op jit(solution)/shard_map/dot_general | solution.py:63
  633.0 0.0 reduce-scatter.5.cloned.1.call-update
  633.0 47.6 %reduce-scatter.5.cloned.1.call-done = f32[16,6144]{1,0:T(8,128)} async-done(((f32[128,6144]{1,0:T(8,128)}), f32[16,6144]{1,0:T(8,128)}) %reduce-scatter.5.cloned.1.call-update) | async-done | bytes 393232 | tf_op jit(solution)/shard_map/reduce_scatter | solution.py:66
  680.6 1.7 convert_element_type.27
  (4 shorter events, 0.0 us)
Async XLA Ops:
  6.5 374.5 %all-gather.5.cloned.1.call-start = ((), (), s32[]{:S(2)}) async-start(), calls=%async_computation.3 | async-start | bytes 40108032 | tf_op jit(solution)/shard_map/all_gather | solution.py:25
  7.3 448.0 %all-gather.7.cloned.1.call-start = ((), (), s32[]{:S(2)}) async-start(), calls=%async_computation.4 | async-start | bytes 1769472 | tf_op jit(solution)/shard_map/all_gather | solution.py:22
  15.3 7.6 %copy-start = (s32[48,8,3]{0,1,2:T(8,128)S(1)}, s32[48,8,3]{0,1,2:T(8,128)}, u32[]{:S(2)}) copy-start(s32[48,8,3]{0,1,2:T(8,128)} %param.7) | copy-start | bytes 13828
  15.3 502.2 %all-to-all-start = ((bf16[16,8,8,6144]{3,2,1,0:T(8,128)(2,1)}), bf16[16,8,8,6144]{3,2,1,0:T(8,128)(2,1)}, u32[]{:S(2)}, u32[]{:S(2)}) async-start(bf16[16,8,8,6144]{3,2,1,0:T(8,128)(2,1)} %stack.2), calls=%async_computation.1 | async-start | bytes 25165824 | tf_op jit(solution)/shard_map/all_to_all | solution.py:14
  22.9 491.6 %reduce-scatter.3.cloned.1.call-start = ((), (), s32[]{:S(2)}) async-start(), calls=%async_computation.5 | async-start | bytes 2359296 | tf_op jit(solution)/shard_map/reduce_scatter | solution.py:31
  455.2 12.6 %copy-start.2 = (bf16[128,6144]{1,0:T(8,128)(2,1)S(1)}, bf16[128,6144]{1,0:T(8,128)(2,1)}, u32[]{:S(2)}) copy-start(bf16[128,6144]{1,0:T(8,128)(2,1)} %all-gather.7.cloned.1.call-done) | copy-start | bytes 4718596
  494.5 22.8 %copy-start.1 = (s32[8,48]{1,0:T(8,128)S(1)}, s32[8,48]{1,0:T(8,128)}, u32[]{:S(2)}) copy-start(s32[8,48]{1,0:T(8,128)} %param.9) | copy-start | bytes 4612
  496.2 71.0 %all-gather.11.cloned.1.call-start = ((), (), s32[]{:S(2)}) async-start(), calls=%async_computation.7 | async-start | bytes 2228224 | tf_op jit(solution)/shard_map/all_gather | solution.py:38
  516.5 102.3 %all-gather.9.cloned.1.call-start = ((), (), s32[]{:S(2)}) async-start(), calls=%async_computation.6 | async-start | bytes 2228224 | tf_op jit(solution)/shard_map/all_gather | solution.py:39
  517.1 163.6 %reduce-scatter.5.cloned.1.call-start = ((), (), s32[]{:S(2)}) async-start(), calls=%async_computation.8 | async-start | bytes 3538944 | tf_op jit(solution)/shard_map/reduce_scatter | solution.py:66
Sparse Core Ops, SparseCore 0:
  9.8 371.2 all-gather.4
  382.9 43.1 all-gather.6
  496.3 18.1 reduce-scatter.2
  516.8 50.2 all-gather.10
  569.4 49.3 all-gather.8
  633.1 47.4 reduce-scatter.4
